TPU v7x, 32 devices: a whole 2x2x4 slice. The times are simulated.
32 devices in a mesh: row: 4 (over y, core), col: 8 (over z, x).
Axes of the slice: x: 2, y: 2, z: 4, core: 2. Of those that a mesh axis runs over, the one named last changes fastest.
Arguments:
- quant_acts: bfloat16 [1024, 8192], P('col', 'row'), may hold values from -6 to 6
- full_acts: bfloat16 [1024, 8192], P('col', 'row'), may hold values from -6 to 6
Outputs:
- hessian: float32 [8192, 8192], P('row', 'col')
- cross_term: float32 [8192, 8192], P('row', 'col')
All inputs are finite; a program needn't handle non-finite values.
Results may differ from a plain program's by a relative error of at most 0.0028.
Values may be sent and summed in bfloat16 or wider, within the bound.
No kernel may reach another device: no remote copies, remote signals or barrier semaphores. Data moves between devices by JAX's collectives and lax.ppermute only.
A program may use at most 64 MiB of HBM per device.

v0:
```python
import jax
import jax.numpy as jnp
from jax import lax
from jax.sharding import PartitionSpec as P


def transposed(left_side, right_side):
    return lax.dot_general(
        left_side, right_side, (((0,), (0,)), ((), ())), preferred_element_type=jnp.float32
    )


def local(quant_acts, full_acts):
    deltas = (full_acts.astype(jnp.float32) - quant_acts.astype(jnp.float32)).astype(jnp.bfloat16)
    slab_wide = lax.all_gather(quant_acts, "row", axis=1, tiled=True)
    column_ops = lax.all_to_all(slab_wide, "col", split_axis=1, concat_axis=0, tiled=True)
    total_tokens = column_ops.shape[0]
    hessian = transposed(lax.all_gather(quant_acts, "col", axis=0, tiled=True), column_ops)
    cross_term = transposed(lax.all_gather(deltas, "col", axis=0, tiled=True), column_ops)
    scale = 1.0 / total_tokens
    return (hessian * scale, cross_term * scale)


def solution(mesh):
    return jax.shard_map(
        local,
        mesh=mesh,
        in_specs=(P("col", "row"), P("col", "row")),
        out_specs=(P("row", "col"), P("row", "col")),
        check_vma=False,
    )
```

profile of v0, /device:TPU:0, one launch (start us, length us, event | category | flops | bytes accessed | tf_op | source)
XLA Modules:
  0.0 229.3 jit_solution(12659035021333383874)
XLA Ops:
  7.2 0.0 all-gather.6.cloned.1.call-start
  7.2 2.0 copy.4
  9.3 0.0 all-gather.6.cloned.1.call-update
  9.3 0.0 all-gather.8.cloned.1.call-start
  9.3 2.1 subtract_convert_fusion
  11.5 0.0 all-gather.8.cloned.1.call-update
  11.5 0.0 all-gather.4.cloned.1.call-start
  11.5 0.7 all-gather.4.cloned.1.call-update
  12.2 23.2 %all-gather.6.cloned.1.call-done = bf16[128,8192]{0,1:T(8,128)(2,1)} async-done(((bf16[128,2048]{0,1:T(8,128)(2,1)}), bf16[128,8192]{0,1:T(8,128)(2,1)}) %all-gather.6.cloned.1.call-update) | async-done | bytes 2097168 | tf_op jit(solution)/shard_map/all_gather | solution.py:15
  35.4 90.8 %all_to_all.19 = bf16[128,8,1024]{0,2,1:T(8,128)(2,1)S(1)} all-to-all(bf16[128,8,1024]{0,2,1:T(8,128)(2,1)} %bitcast.8), channel_id=1, replica_groups=mesh['row'=4,'col'=8] {'col'}, dimensions={1} | all-to-all | bytes 4194304 | tf_op jit(solution)/shard_map/all_to_all | solution.py:16
  126.3 2.6 %copy.5 = bf16[8,128,1024]{2,1,0:T(8,128)(2,1)} copy(bf16[8,128,1024]{1,2,0:T(8,128)(2,1)S(1)} %bitcast.7) | data formatting | bytes 4194304 | tf_op jit(solution)/shard_map/all_to_all | solution.py:16
  128.8 11.7 %all-gather.8.cloned.1.call-done = bf16[1024,2048]{1,0:T(8,128)(2,1)} async-done(((bf16[128,2048]{1,0:T(8,128)(2,1)}), bf16[1024,2048]{1,0:T(8,128)(2,1)}) %all-gather.8.cloned.1.call-update) | async-done | bytes 4194320 | tf_op jit(solution)/shard_map/all_gather | solution.py:19
  140.6 0.0 copy-start
  140.6 11.0 %convolution_multiply_fusion = f32[2048,1024]{1,0:T(8,128)} fusion(bf16[1024,2048]{1,0:T(8,128)(2,1)} %all-gather.8.cloned.1.call-done, bf16[1024,1024]{1,0:T(8,128)(2,1)} %bitcast.9), kind=kOutput, calls=%fused_computation | convolution fusion | flops 4297064448 | bytes 14680064 | tf_op jit(solution)/shard_map/dot_general | solution.py:8
  151.5 62.2 %all-gather.4.cloned.1.call-done = bf16[1024,2048]{1,0:T(8,128)(2,1)} async-done(((bf16[128,2048]{1,0:T(8,128)(2,1)}), bf16[1024,2048]{1,0:T(8,128)(2,1)}) %all-gather.4.cloned.1.call-update) | async-done | bytes 4194320 | tf_op jit(solution)/shard_map/all_gather | solution.py:18
  213.8 0.0 copy-done
  213.8 9.0 %convolution_multiply_fusion.1 = f32[2048,1024]{1,0:T(8,128)} fusion(bf16[1024,2048]{1,0:T(8,128)(2,1)} %all-gather.4.cloned.1.call-done, bf16[1024,1024]{1,0:T(8,128)(2,1)S(1)} %bitcast.10), kind=kOutput, calls=%fused_computation.1 | convolution fusion | flops 4297064448 | bytes 14680064 | tf_op jit(solution)/shard_map/dot_general | solution.py:8
Async XLA Ops:
  7.2 28.3 %all-gather.6.cloned.1.call-start = ((), (), s32[]{:S(2)}) async-start(), calls=%async_computation.2 | async-start | bytes 2621440 | tf_op jit(solution)/shard_map/all_gather | solution.py:15
  9.3 131.3 %all-gather.8.cloned.1.call-start = ((), (), s32[]{:S(2)}) async-start(), calls=%async_computation.3 | async-start | bytes 4718592 | tf_op jit(solution)/shard_map/all_gather | solution.py:19
  11.5 202.3 %all-gather.4.cloned.1.call-start = ((), (), s32[]{:S(2)}) async-start(), calls=%async_computation.1 | async-start | bytes 4718592 | tf_op jit(solution)/shard_map/all_gather | solution.py:18
  140.6 73.2 %copy-start = (bf16[8,128,1024]{2,1,0:T(8,128)(2,1)S(1)}, bf16[8,128,1024]{2,1,0:T(8,128)(2,1)}, u32[]{:S(2)}) copy-start(bf16[8,128,1024]{2,1,0:T(8,128)(2,1)} %copy.5) | copy-start | bytes 6291460
Sparse Core Ops, SparseCore 0:
  10.1 25.2 all-gather.5
  37.6 102.9 all-gather.7
  142.7 71.0 all-gather.3
where the time goes:
time: 230 us; the launch traced here: 229 us
  waiting for transfers between devices  97.9 us (43%)
  blocking collectives  90.8 us (39%)
  matrix products  20 us (9%)
  between operations  13.7 us (6%)
  local copies, waits for them, and re-layouts  4.63 us (2%)
    all_to_all x1, blocking collectives, local(): lax.all_to_all(slab_wide, 'col', split_axis=1, concat_axis=0, tiled=True)  90.8 us
    all_gather x1, waiting for transfers between devices, local(): lax.all_gather(quant_acts, 'col', axis=0, tiled=True)  62.2 us
    all_gather x1, waiting for transfers between devices, local(): slab_wide = lax.all_gather(quant_acts, 'row', axis=1, tiled=True)  23.2 us
    dot_general x2, matrix products, transposed(): lax.dot_general(left_side, right_side, (((0,), (0,)), ((), ())), preferre...  20 us
    all_gather x1, waiting for transfers between devices, local(): lax.all_gather(deltas, 'col', axis=0, tiled=True)  11.7 us
  transfers between devices with their start and end apart: 3, of which 3 were waited for; matrix products, arithmetic and copies ran while one was open for 7% of the time, Pallas kernels for 0%

commit v1 on v0

--- a/solution.py
+++ b/solution.py
@@ -2,6 +2,12 @@
 import jax.numpy as jnp
 from jax import lax
 from jax.sharding import PartitionSpec as P
+
+
+def trade_parts(x, axis, split, join):
+    shards = jnp.split(x, lax.axis_size(axis), axis=split)
+    received = lax.all_to_all(jnp.stack(shards), axis, 0, 0)
+    return jnp.concatenate(received, axis=join)
 
 
 def transposed(left_side, right_side):
@@ -13,7 +19,7 @@
 def local(quant_acts, full_acts):
     deltas = (full_acts.astype(jnp.float32) - quant_acts.astype(jnp.float32)).astype(jnp.bfloat16)
     slab_wide = lax.all_gather(quant_acts, "row", axis=1, tiled=True)
-    column_ops = lax.all_to_all(slab_wide, "col", split_axis=1, concat_axis=0, tiled=True)
+    column_ops = trade_parts(slab_wide, "col", 1, 0)
     total_tokens = column_ops.shape[0]
     hessian = transposed(lax.all_gather(quant_acts, "col", axis=0, tiled=True), column_ops)
     cross_term = transposed(lax.all_gather(deltas, "col", axis=0, tiled=True), column_ops)

time: 230 us -> 235 us (1.022)
  local copies, waits for them, and re-layouts: 4.63 us -> 17.1 us
  waiting for transfers between devices: 97.9 us -> 86.7 us
  blocking collectives: 90.8 us -> 96.7 us
    all_gather x1, waiting for transfers between devices: 62.2 us -> 5.82 us  [local(): lax.all_gather(quant_acts, 'col', axis=0, tiled=True)]
    all_gather x1, waiting for transfers between devices: 11.7 us -> 55.5 us  [local(): lax.all_gather(deltas, 'col', axis=0, tiled=True)]
    unnamed x3 -> x8, local copies, waits for them, and re-layouts: 2.05 us -> 16.1 us
    all_to_all x1, blocking collectives: 90.8 us -> 96.7 us  [trade_parts(): received = lax.all_to_all(jnp.stack(shards), axis, 0, 0)]
    all_to_all x1 -> x0, local copies, waits for them, and re-layouts: 2.58 us -> none  [local(): lax.all_to_all(slab_wide, 'col', split_axis=1, concat_axis=0, tiled=True)]
  transfers between devices with their start and end apart: 3 -> 3, of which waited for: 3 -> 3; matrix products, arithmetic and copies ran while one was open for 7% -> 12% of each run, Pallas kernels for 0% -> 0%
where the time goes in v1:
time: 235 us
  blocking collectives  96.7 us (41%)
  waiting for transfers between devices  86.7 us (37%)
  matrix products  18 us (8%)
  local copies, waits for them, and re-layouts  17.1 us (7%)
  between operations  13.8 us (6%)
    all_to_all x1, blocking collectives, trade_parts(): received = lax.all_to_all(jnp.stack(shards), axis, 0, 0)  96.7 us
    all_gather x1, waiting for transfers between devices, local(): lax.all_gather(deltas, 'col', axis=0, tiled=True)  55.5 us
    all_gather x1, waiting for transfers between devices, local(): slab_wide = lax.all_gather(quant_acts, 'row', axis=1, tiled=True)  24 us
    dot_general x2, matrix products, transposed(): lax.dot_general(left_side, right_side, (((0,), (0,)), ((), ())), preferre...  18 us
    unnamed x8, local copies, waits for them, and re-layouts  16.1 us
    all_gather x1, waiting for transfers between devices, local(): lax.all_gather(quant_acts, 'col', axis=0, tiled=True)  5.82 us
  transfers between devices with their start and end apart: 3, of which 3 were waited for; matrix products, arithmetic and copies ran while one was open for 12% of the time, Pallas kernels for 0%

profile of v1, /device:TPU:0, one launch (start us, length us, event | category | flops | bytes accessed | tf_op | source)
XLA Modules:
  0.0 234.5 jit_solution(18279411959545005860)
XLA Ops:
  7.2 0.0 all-gather.4.cloned.1.call-start
  7.2 0.7 all-gather.4.cloned.1.call-update
  7.9 0.0 all-gather.6.cloned.1.call-start
  7.9 0.7 all-gather.6.cloned.1.call-update
  8.6 0.0 all-gather.8.cloned.1.call-start
  8.7 2.1 subtract_convert_fusion
  10.8 0.0 all-gather.8.cloned.1.call-update
  10.9 24.0 %all-gather.4.cloned.1.call-done = bf16[128,8192]{1,0:T(8,128)(2,1)} async-done(((bf16[128,2048]{1,0:T(8,128)(2,1)}), bf16[128,8192]{1,0:T(8,128)(2,1)}) %all-gather.4.cloned.1.call-update) | async-done | bytes 2097168 | tf_op jit(solution)/shard_map/all_gather | solution.py:21
  34.9 1.0 fusion.7
  35.8 1.0 fusion.6
  36.8 1.0 fusion.5
  37.8 1.0 fusion.4
  38.7 1.0 fusion.3
  39.7 1.0 fusion.2
  40.7 1.0 fusion.1
  41.7 1.0 fusion
  42.6 96.7 %all_to_all.5 = bf16[8,128,1024]{2,1,0:T(8,128)(2,1)S(1)} all-to-all(bf16[8,128,1024]{2,1,0:T(8,128)(2,1)S(1)} %fusion), channel_id=1, replica_groups=mesh['row'=4,'col'=8] {'col'}, dimensions={0} | all-to-all | bytes 4194304 | tf_op jit(solution)/shard_map/all_to_all | solution.py:9
  139.3 5.8 %all-gather.6.cloned.1.call-done = bf16[1024,2048]{1,0:T(8,128)(2,1)} async-done(((bf16[128,2048]{1,0:T(8,128)(2,1)}), bf16[1024,2048]{1,0:T(8,128)(2,1)}) %all-gather.6.cloned.1.call-update) | async-done | bytes 4194320 | tf_op jit(solution)/shard_map/all_gather | solution.py:24
  145.2 9.0 %multiply_bitcast_fusion = f32[2048,1024]{0,1:T(8,128)} fusion(bf16[1024,1024]{1,0:T(8,128)(2,1)S(1)} %bitcast.39, bf16[1024,2048]{1,0:T(8,128)(2,1)} %all-gather.6.cloned.1.call-done), kind=kOutput, calls=%fused_computation | convolution fusion | flops 4297064448 | bytes 14680064 | tf_op jit(solution)/shard_map/dot_general | solution.py:14
  154.2 9.3 %copy.4 = f32[2048,1024]{1,0:T(8,128)} copy(f32[2048,1024]{0,1:T(8,128)} %multiply_bitcast_fusion) | data formatting | bytes 16777216
  163.5 55.5 %all-gather.8.cloned.1.call-done = bf16[1024,2048]{1,0:T(8,128)(2,1)} async-done(((bf16[128,2048]{1,0:T(8,128)(2,1)}), bf16[1024,2048]{1,0:T(8,128)(2,1)}) %all-gather.8.cloned.1.call-update) | async-done | bytes 4194320 | tf_op jit(solution)/shard_map/all_gather | solution.py:25
  219.0 9.0 %convolution_multiply_fusion = f32[2048,1024]{1,0:T(8,128)} fusion(bf16[1024,2048]{1,0:T(8,128)(2,1)} %all-gather.8.cloned.1.call-done, bf16[1024,1024]{1,0:T(8,128)(2,1)S(1)} %bitcast.40), kind=kOutput, calls=%fused_computation.1 | convolution fusion | flops 4297064448 | bytes 14680064 | tf_op jit(solution)/shard_map/dot_general | solution.py:14
Async XLA Ops:
  7.2 27.7 %all-gather.4.cloned.1.call-start = ((), (), s32[]{:S(2)}) async-start(), calls=%async_computation.1 | async-start | bytes 2621440 | tf_op jit(solution)/shard_map/all_gather | solution.py:21
  7.9 137.3 %all-gather.6.cloned.1.call-start = ((), (), s32[]{:S(2)}) async-start(), calls=%async_computation.2 | async-start | bytes 4718592 | tf_op jit(solution)/shard_map/all_gather | solution.py:24
  8.6 210.4 %all-gather.8.cloned.1.call-start = ((), (), s32[]{:S(2)}) async-start(), calls=%async_computation.3 | async-start | bytes 4718592 | tf_op jit(solution)/shard_map/all_gather | solution.py:25
Sparse Core Ops, SparseCore 0:
  9.5 25.2 all-gather.3
  37.0 108.1 all-gather.5
  147.3 71.6 all-gather.7
